TPU v7x, 32 devices: a whole 2x2x4 slice. The times are simulated.
32 devices in a mesh: branch: 4 (over z), seq: 2 (over x), rep: 4 (over y, core).
Axes of the slice: x: 2, y: 2, z: 4, core: 2. Of those that a mesh axis runs over, the one named last changes fastest.
Arguments:
- noisy: bfloat16 [4, 1024, 5120], P('rep'), may hold values from -6 to 6
- generated: bfloat16 [4, 1024, 5120], P('rep', 'seq'), may hold values from -170 to 170
- caption: bfloat16 [4, 5120], P('rep'), may hold values from -0.59765625 to 0.59765625
- null_caption: bfloat16 [5120], replicated, may hold values from -0.59765625 to 0.59765625
- caption_drop: int32 [4], P('rep'), may hold values from 0 to 1, as said below
- timestep: int32 [4], P('rep'), may hold values from 0 to 999
- window_start: int32 [4], P('rep'), may hold values from 0 to 31736
- teacher_qkv: bfloat16 [3, 5120, 1024], P(None, None, ('branch', 'seq')), may hold values from -0.078125 to 0.078125
- teacher_out: bfloat16 [1024, 5120], P(('branch', 'seq')), may hold values from -0.1875 to 0.1875
- teacher_gain: float32 [5120], replicated, may hold values from 0.5 to 1.5
- teacher_qk_gain: float32 [2, 1024], P(None, ('branch', 'seq')), may hold values from 0.7 to 2.6
- critic_qkv: bfloat16 [3, 5120, 1024], P(None, None, ('branch', 'seq')), may hold values from -0.078125 to 0.078125
- critic_out: bfloat16 [1024, 5120], P(('branch', 'seq')), may hold values from -0.1875 to 0.1875
- critic_gain: float32 [5120], replicated, may hold values from 0.5 to 1.5
- critic_qk_gain: float32 [2, 1024], P(None, ('branch', 'seq')), may hold values from 0.7 to 2.6
Outputs:
- generator_grad: bfloat16 [4, 1024, 5120], P('rep', 'seq')
- critic_qkv_grad: float32 [3, 5120, 1024], P(None, 'rep', ('branch', 'seq'))
- critic_out_grad: float32 [1024, 5120], P(('branch', 'seq'), 'rep')
Inputs may be any that keep to these rules, and one draw needn't show every extreme that they name: `caption_drop`: each window's flag is drawn independently.
All inputs are finite; a program needn't handle non-finite values. Where the computation divides by a largest or mean magnitude, that divisor is 1e-20 or more.
Results may differ from a plain program's by a relative error of at most 0.018.
The roundings to bfloat16 on the way count: a program that leaves them out, or rounds other values in their place, can miss the bound.
Values may be sent and summed in bfloat16 or wider, within the bound.
No kernel may reach another device: no remote copies, remote signals or barrier semaphores. Data moves between devices by JAX's collectives and lax.ppermute only.
A program may use at most 192 MiB of HBM per device.

v0:
```python
import jax
import jax.numpy as jnp
from jax import lax
from jax.sharding import PartitionSpec as P

LEN = 1024
GRID_H = 30
GRID_W = 52
guidance = 5.0
score_scale = 128.0 ** (-0.5)
norm_eps = 1e-06


def rope_tables(first_token):
    token_index = first_token + jnp.arange(LEN, dtype=jnp.int32)
    plane_size = GRID_H * GRID_W
    frame_index = token_index // plane_size
    remainder = token_index - frame_index * plane_size
    row_index = remainder // GRID_W
    column_index = remainder - row_index * GRID_W
    pair_index = jnp.arange(64, dtype=jnp.int32)
    in_frames = pair_index < 22
    in_rows = jnp.logical_and(pair_index >= 22, pair_index < 43)
    local_rank = jnp.where(
        in_frames, pair_index, jnp.where(in_rows, pair_index - 22, pair_index - 43)
    ).astype(jnp.float32)
    axis_width = jnp.where(in_frames, 44.0, 42.0).astype(jnp.float32)
    frequency = jnp.exp(-jnp.log(10000.0) * 2.0 * local_rank / axis_width)
    chosen = jnp.where(
        in_frames[None, :],
        frame_index[:, None],
        jnp.where(in_rows[None, :], row_index[:, None], column_index[:, None]),
    ).astype(jnp.float32)
    angles = chosen * frequency[None, :]
    angles = jnp.concatenate([angles, angles], axis=1)
    return (jnp.cos(angles), jnp.sin(angles))


def rotate_half(values):
    return jnp.concatenate([-values[..., 64:], values[..., :64]], axis=-1)


def rotate_back(values):
    return jnp.concatenate([values[..., 64:], -values[..., :64]], axis=-1)


def norm_tokens(inputs, gain_values):
    scaled = (
        inputs
        * lax.rsqrt(jnp.mean(inputs * inputs, axis=-1, keepdims=True) + norm_eps)
        * gain_values
    )
    return scaled.astype(jnp.bfloat16)


def undo_norm(raw_values, inverse, gain_values, grad_normed):
    scaled = gain_values * grad_normed
    return inverse * scaled - raw_values * inverse * inverse * inverse * jnp.mean(
        scaled * raw_values, axis=-1, keepdims=True
    )


def head_forward(hidden, weights, qk_gains, cosine_table, sine_table):
    projected = jnp.einsum("bsd,kdc->kbsc", hidden, weights, preferred_element_type=jnp.float32)
    batch_size = hidden.shape[0]
    length = hidden.shape[1]
    query_raw = projected[0].reshape(batch_size, length, -1, 128)
    key_raw = projected[1].reshape(batch_size, length, -1, 128)
    value_rows = projected[2].reshape(batch_size, length, -1, 128).astype(jnp.bfloat16)
    gain_query = qk_gains[0].reshape(-1, 128)
    gain_key = qk_gains[1].reshape(-1, 128)
    inv_query = lax.rsqrt(jnp.mean(query_raw * query_raw, axis=-1, keepdims=True) + norm_eps)
    inv_key = lax.rsqrt(jnp.mean(key_raw * key_raw, axis=-1, keepdims=True) + norm_eps)
    normed_query = query_raw * inv_query * gain_query
    normed_key = key_raw * inv_key * gain_key
    cosine_h = cosine_table[:, :, None, :]
    sine_h = sine_table[:, :, None, :]
    rope_query = (normed_query * cosine_h + rotate_half(normed_query) * sine_h).astype(jnp.bfloat16)
    rope_key = (normed_key * cosine_h + rotate_half(normed_key) * sine_h).astype(jnp.bfloat16)
    scores = (
        jnp.einsum("bqhe,bkhe->bhqk", rope_query, rope_key, preferred_element_type=jnp.float32)
        * score_scale
    )
    exponent = jnp.exp(scores)
    probability = exponent / jnp.sum(exponent, axis=-1, keepdims=True)
    prob_rounded = probability.astype(jnp.bfloat16)
    attended = jnp.einsum(
        "bhqk,bkhe->bqhe", prob_rounded, value_rows, preferred_element_type=jnp.float32
    )
    attended = attended.astype(jnp.bfloat16).reshape(batch_size, length, -1)
    saved_state = (
        query_raw,
        key_raw,
        inv_query,
        inv_key,
        rope_query,
        rope_key,
        value_rows,
        probability,
        prob_rounded,
    )
    return (attended, saved_state)


def head_backward(hidden, grad_attn, saved_state, qk_gains, cosine_table, sine_table):
    (
        query_raw,
        key_raw,
        inv_query,
        inv_key,
        rope_query,
        rope_key,
        value_rows,
        probability,
        prob_rounded,
    ) = saved_state
    batch_size = hidden.shape[0]
    length = hidden.shape[1]
    grad_heads = grad_attn.reshape(batch_size, length, -1, 128)
    grad_prob = jnp.einsum(
        "bqhe,bkhe->bhqk", grad_heads, value_rows, preferred_element_type=jnp.float32
    )
    grad_score = (
        probability
        * (grad_prob - jnp.sum(grad_prob * probability, axis=-1, keepdims=True))
        * score_scale
    )
    grad_score = grad_score.astype(jnp.bfloat16)
    grad_qrot = jnp.einsum(
        "bhqk,bkhe->bqhe", grad_score, rope_key, preferred_element_type=jnp.float32
    )
    grad_krot = jnp.einsum(
        "bhqk,bqhe->bkhe", grad_score, rope_query, preferred_element_type=jnp.float32
    )
    grad_value = jnp.einsum(
        "bhqk,bqhe->bkhe", prob_rounded, grad_heads, preferred_element_type=jnp.float32
    )
    cosine_h = cosine_table[:, :, None, :]
    sine_h = sine_table[:, :, None, :]
    grad_qnorm = grad_qrot * cosine_h + rotate_back(grad_qrot * sine_h)
    grad_knorm = grad_krot * cosine_h + rotate_back(grad_krot * sine_h)
    grad_query = undo_norm(query_raw, inv_query, qk_gains[0].reshape(-1, 128), grad_qnorm)
    grad_key = undo_norm(key_raw, inv_key, qk_gains[1].reshape(-1, 128), grad_knorm)
    grad_stack = jnp.stack(
        [
            grad_query.reshape(batch_size, length, -1),
            grad_key.reshape(batch_size, length, -1),
            grad_value.reshape(batch_size, length, -1),
        ]
    ).astype(jnp.bfloat16)
    return jnp.einsum("bsd,kbsc->kdc", hidden, grad_stack, preferred_element_type=jnp.float32)


def body(
    noisy,
    generated,
    caption,
    null_caption,
    caption_drop,
    timestep,
    window_start,
    teacher_qkv,
    teacher_out,
    teacher_gain,
    teacher_qk_gain,
    critic_qkv,
    critic_out,
    critic_gain,
    critic_qk_gain,
):
    length = noisy.shape[1]
    width = noisy.shape[2]
    fraction = (timestep.astype(jnp.float32) + 1.0) / 1001.0
    noise_level = (5.0 * fraction / (1.0 + 4.0 * fraction))[:, None, None]
    used_caption = jnp.where(caption_drop[:, None] == 1, null_caption[None, :], caption)
    cond_shift = used_caption.astype(jnp.float32)[:, None, :]
    null_shift = null_caption.astype(jnp.float32)[None, None, :]
    latent = noisy.astype(jnp.float32)
    cond_normed = norm_tokens(latent + cond_shift, teacher_gain)
    null_normed = norm_tokens(latent + null_shift, teacher_gain)
    critic_normed = norm_tokens(latent + cond_shift, critic_gain)
    cosine_table, sine_table = jax.vmap(rope_tables)(window_start)
    cond_attn, unused = head_forward(
        cond_normed, teacher_qkv, teacher_qk_gain, cosine_table, sine_table
    )
    null_attn, unused = head_forward(
        null_normed, teacher_qkv, teacher_qk_gain, cosine_table, sine_table
    )
    fake_attn, saved_state = head_forward(
        critic_normed, critic_qkv, critic_qk_gain, cosine_table, sine_table
    )
    share_rows = length // lax.axis_size("seq")
    row_start = lax.axis_index("seq") * share_rows
    target = generated.astype(jnp.float32)
    cond_part = jnp.einsum(
        "bsc,cd->sbd", cond_attn, teacher_out, preferred_element_type=jnp.float32
    )
    null_part = jnp.einsum(
        "bsc,cd->sbd", null_attn, teacher_out, preferred_element_type=jnp.float32
    )
    guided_seq = lax.psum_scatter(
        (guidance * cond_part - (guidance - 1.0) * null_part).astype(jnp.bfloat16),
        "seq",
        scatter_dimension=0,
        tiled=True,
    )
    guided_rows = jnp.transpose(lax.psum(guided_seq, "branch").astype(jnp.float32), (1, 0, 2))
    fake_local = jnp.einsum(
        "bsc,cd->bsd", fake_attn, critic_out, preferred_element_type=jnp.float32
    )
    fake_full = lax.psum(fake_local.astype(jnp.bfloat16), ("branch", "seq")).astype(jnp.float32)
    target_full = lax.all_gather(generated, "seq", axis=1, tiled=True).astype(jnp.float32)
    fake_rows = lax.dynamic_slice_in_dim(fake_full, row_start, share_rows, 1)
    latent_rows = lax.dynamic_slice_in_dim(latent, row_start, share_rows, 1)
    cond_rows = latent_rows + cond_shift
    null_rows = latent_rows + null_shift
    real_velocity = guidance * cond_rows - (guidance - 1.0) * null_rows + guided_rows
    fake_velocity = cond_rows + fake_rows
    real_pred = latent_rows - noise_level * real_velocity
    fake_pred = latent_rows - noise_level * fake_velocity
    fake_pred_full = latent - noise_level * (latent + cond_shift + fake_full)
    cotangent = (-noise_level * (fake_pred_full - target_full) / 64.0).astype(jnp.bfloat16)
    out_grads = jnp.einsum("bsc,bsd->cd", fake_attn, cotangent, preferred_element_type=jnp.float32)
    grad_attn = jnp.einsum(
        "bsd,cd->bsc", cotangent, critic_out, preferred_element_type=jnp.float32
    ).astype(jnp.bfloat16)
    abs_total = lax.psum(jnp.sum(jnp.abs(real_pred - target), axis=(1, 2)), "seq")
    spread = abs_total / (length * width)
    generator_grad = ((fake_pred - real_pred) / (spread[:, None, None] + 1e-05)).astype(
        jnp.bfloat16
    )
    proj_share, out_share = (
        lax.psum_scatter(
            head_backward(
                critic_normed, grad_attn, saved_state, critic_qk_gain, cosine_table, sine_table
            ).astype(jnp.bfloat16),
            "rep",
            scatter_dimension=1,
            tiled=True,
        ).astype(jnp.float32),
        lax.psum_scatter(
            out_grads.astype(jnp.bfloat16), "rep", scatter_dimension=1, tiled=True
        ).astype(jnp.float32),
    )
    return (generator_grad, proj_share, out_share)


def solution(mesh):
    in_specs = (
        P("rep", None, None),
        P("rep", "seq", None),
        P("rep", None),
        P(),
        P("rep"),
        P("rep"),
        P("rep"),
        P(None, None, ("branch", "seq")),
        P(("branch", "seq"), None),
        P(),
        P(None, ("branch", "seq")),
        P(None, None, ("branch", "seq")),
        P(("branch", "seq"), None),
        P(),
        P(None, ("branch", "seq")),
    )
    out_specs = (
        P("rep", "seq", None),
        P(None, "rep", ("branch", "seq")),
        P(("branch", "seq"), "rep"),
    )
    return jax.shard_map(body, mesh=mesh, in_specs=in_specs, out_specs=out_specs, check_vma=False)
```

profile of v0, /device:TPU:0, one launch (start us, length us, event | category | flops | bytes accessed | tf_op | source)
XLA Modules:
  0.0 812.3 jit_solution(154347781953120975)
XLA Ops:
  10.1 6.3 copy.18
  16.6 11.9 %multiply_reduce_fusion = (f32[1024]{0:T(1024)S(1)}, f32[1024]{0:T(1024)S(1)}) fusion(bf16[1,1024,5120]{2,1,0:T(8,128)(2,1)} %param.15, f32[5120]{0:T(1024)S(1)} %convert_element_type.334, f32[5120]{0:T(1024)S(1)} %bitcast.380), kind=kLoop, calls=%fused_computation.3 | loop fusion | flops 36698112 | bytes 10534912 | tf_op jit(solution)/shard_map/reduce_sum | solution.py:50
  28.5 6.9 fusion.10
  38.7 4.3 fusion.26
  46.7 5.8 convert_bitcast_fusion
  52.6 6.4 copy.20
  59.0 10.0 %fusion.5 = f32[1024,384]{0,1:S(1)} fusion(bf16[5120,384]{0,1:T(8,128)(2,1)} %bitcast.378, bf16[1,1024,5120]{2,1,0:T(8,128)(2,1)} %param.15, f32[1024]{0:T(1024)S(1)} %add_rsqrt_fusion.2, f32[5120]{0:T(1024)S(1)} %convert_element_type.334, f32[5120]{0:T(1024)S(1)} %copy-done.31), kind=kOutput, calls=%fused_computation.12 | convolution fusion | flops 4052746240 | bytes 16035840
  69.2 4.3 fusion.2
  74.9 6.2 fusion.28
  81.1 6.4 fusion.27
  87.5 11.7 %fusion.36 = f32[1024,5120]{1,0:T(8,128)} fusion(bf16[128,5120]{1,0:T(8,128)(2,1)S(1)} %copy-done, f32[1024,1024]{0,1:T(8,128)} %get-tuple-element.54, f32[1024]{0:T(1024)S(1)} %get-tuple-element.53, f32[3,1,1024,128]{2,3,1,0:T(8,128)} %bitcast.375), kind=kOutput, calls=%fused_computation.55 | convolution fusion | flops 1613889536 | bytes 26742784 | tf_op jit(solution)/shard_map/bsc,cd->sbd/dot_general | solution.py:195
  99.2 12.8 %fusion.18 = bf16[1024,1,5120]{2,0,1:T(8,128)(2,1)} fusion(bf16[128,5120]{1,0:T(8,128)(2,1)S(1)} %copy-done, f32[1024,5120]{1,0:T(8,128)} %fusion.36, f32[1024,1024]{0,1:T(8,128)} %get-tuple-element.56, f32[1024]{0:T(1024)S(1)} %get-tuple-element.55, f32[3,1,1024,128]{2,3,1,0:T(8,128)S(1)} %bitcast.371), kind=kOutput, calls=%fused_computation.28 | convolution fusion | flops 1634861056 | bytes 37228544 | tf_op jit(solution)/shard_map/bsc,cd->sbd/dot_general | solution.py:198
  112.8 30.1 %all-gather.2.cloned.1.call-done = bf16[1,1024,5120]{2,1,0:T(8,128)(2,1)} async-done(((bf16[1,512,5120]{2,1,0:T(8,128)(2,1)}), bf16[1,1024,5120]{2,1,0:T(8,128)(2,1)}) %all-gather.2.cloned.1.call-update) | async-done | bytes 10485776 | tf_op jit(solution)/shard_map/all_gather | solution.py:212
  143.0 339.1 %all-reduce.3.cloned.1.call-done = bf16[1,1024,5120]{2,1,0:T(8,128)(2,1)} async-done(((bf16[1,1024,5120]{2,1,0:T(8,128)(2,1)}), bf16[1,1024,5120]{2,1,0:T(8,128)(2,1)}) %all-reduce.3.cloned.1.call-update) | async-done | bytes 10485776 | tf_op jit(solution)/shard_map/psum | solution.py:211
  482.1 13.9 %fusion.7 = bf16[1024,5120]{1,0:T(8,128)(2,1)S(1)} fusion(bf16[1,1024,5120]{2,1,0:T(8,128)(2,1)} %all-gather.2.cloned.1.call-done, bf16[1,1024,5120]{2,1,0:T(8,128)(2,1)} %param.15, f32[]{:T(128)} %bitcast, f32[]{:T(128)} %bitcast.92, f32[5120]{0:T(1024)S(1)} %bitcast.383, bf16[1,1024,5120]{2,1,0:T(8,128)(2,1)} %all-reduce.3.cloned.1.call-done), kind=kLoop, calls=%fused_computation.13 | loop fusion | flops 57671680 | bytes 41963528 | tf_op jit(solution)/shard_map/reshape.74
  503.6 3.9 fusion.85
  521.8 6.2 fusion.22
  528.6 13.9 %convert_element_type.317 = f32[1,1024,5120]{2,1,0:T(8,128)} convert(bf16[1,1024,5120]{2,1,0:T(8,128)(2,1)} %param.15) | non-fusion elementwise | flops 5242880 | bytes 31457280 | tf_op jit(solution)/shard_map/convert_element_type | solution.py:178
  542.5 14.5 %convert_element_type.333 = f32[1,1024,5120]{2,1,0:T(8,128)} convert(bf16[1,1024,5120]{2,1,0:T(8,128)(2,1)} %all-reduce.3.cloned.1.call-done) | non-fusion elementwise | flops 5242880 | bytes 31457280 | tf_op jit(solution)/shard_map/convert_element_type | solution.py:211
  558.8 25.3 %reduce-scatter.6.cloned.1.call-done = bf16[3,1280,128]{1,2,0:T(8,128)(2,1)} async-done(((bf16[3,5120,128]{1,2,0:T(8,128)(2,1)}), bf16[3,1280,128]{1,2,0:T(8,128)(2,1)}) %reduce-scatter.6.cloned.1.call-update) | async-done | bytes 983056 | tf_op jit(solution)/shard_map/reduce_scatter | solution.py:233
  586.9 188.4 %all-reduce.5.cloned.1.call-done = bf16[1,512,5120]{2,1,0:T(8,128)(2,1)} async-done(((bf16[1,512,5120]{2,1,0:T(8,128)(2,1)}), bf16[1,512,5120]{2,1,0:T(8,128)(2,1)}) %all-reduce.5.cloned.1.call-update) | async-done | bytes 5242896 | tf_op jit(solution)/shard_map/psum | solution.py:207
  775.3 9.9 %abs_reduce_fusion = f32[]{:T(128)} fusion(bf16[1,512,5120]{2,1,0:T(8,128)(2,1)} %param.16, bf16[1,512,5120]{2,1,0:T(8,128)(2,1)} %all-reduce.5.cloned.1.call-done, f32[5120]{0:T(1024)S(1)} %convert_element_type.334, f32[5120]{0:T(1024)S(1)} %bitcast.385, f32[]{:T(128)} %bitcast, f32[1,1024,5120]{2,1,0:T(8,128)} %convert_element_type.317, s32[]{:T(128)S(6)} %select_n.143), kind=kLoop, calls=%fused_computation.19 | loop fusion | flops 34078720 | bytes 21012492 | tf_op jit(solution)/shard_map/reduce_sum | solution.py:227
  785.2 5.5 psum.23
  791.4 13.3 %divide_convert_fusion = bf16[1,512,5120]{2,1,0:T(8,128)(2,1)} fusion(f32[1,1024,5120]{2,1,0:T(8,128)} %convert_element_type.333, s32[]{:T(128)S(6)} %select_n.143, f32[1,1024,5120]{2,1,0:T(8,128)} %convert_element_type.317, f32[]{:T(128)} %bitcast.88, f32[5120]{0:T(1024)S(1)} %bitcast.386, f32[]{:T(128)} %bitcast, ...), kind=kLoop, calls=%fused_computation.18 | loop fusion | flops 39321600 | bytes 31498252 | tf_op jit(solution)/shard_map/convert_element_type | solution.py:229
  (138 shorter events, 36.0 us)
Async XLA Ops:
  8.0 79.5 %copy-start = (bf16[128,5120]{1,0:T(8,128)(2,1)S(1)}, bf16[128,5120]{1,0:T(8,128)(2,1)}, u32[]{:S(2)}) copy-start(bf16[128,5120]{1,0:T(8,128)(2,1)} %param.23) | copy-start | bytes 3932164
  8.0 134.9 %all-gather.2.cloned.1.call-start = ((), (), s32[]{:S(2)}) async-start(), calls=%async_computation.6 | async-start | bytes 15728640 | tf_op jit(solution)/shard_map/all_gather | solution.py:212
  8.8 7.7 copy-start.28
  8.8 473.3 %all-reduce.3.cloned.1.call-start = ((), (), s32[]{:S(2)}) async-start(), calls=%async_computation.3 | async-start | bytes 20971520 | tf_op jit(solution)/shard_map/psum | solution.py:211
  16.6 11.9 %copy-start.2 = (bf16[1,1024,5120]{2,1,0:T(8,128)(2,1)S(1)}, bf16[1,1024,5120]{2,1,0:T(8,128)(2,1)}, u32[]{:S(2)}) copy-start(bf16[1,1024,5120]{2,1,0:T(8,128)(2,1)} %param.15) | copy-start | bytes 31457284
  16.6 11.9 %copy-start.32 = (f32[5120]{0:T(1024)S(1)}, f32[5120]{0:T(1024)}, u32[]{:S(2)}) copy-start(f32[5120]{0:T(1024)} %param.28) | copy-start | bytes 61444
  28.5 7.0 copy-start.29
  35.4 7.6 copy-start.3
  36.7 6.3 copy-start.7
  52.5 6.5 copy-start.31
  52.5 475.6 %reduce-scatter.4.cloned.1.call-start = ((), (), s32[]{:S(2)}) async-start(), calls=%async_computation.4 | async-start | bytes 15728640 | tf_op jit(solution)/shard_map/reduce_scatter | solution.py:201
  52.6 16.6 %slice-start = ((s8[10485760]{0:T(1024)(128)(4,1)}), s8[2097152]{0:T(1024)(128)(4,1)S(1)}, s32[]{:S(2)}) async-start(s8[10485760]{0:T(1024)(128)(4,1)} %bitcast.350), calls=%async_computation.9 | async-start | bytes 4194304
  59.0 10.2 %slice-start.1 = ((s8[10485760]{0:T(1024)(128)(4,1)}), s8[4194304]{0:T(1024)(128)(4,1)S(1)}, s32[]{:S(2)}) async-start(s8[10485760]{0:T(1024)(128)(4,1)} %bitcast.350), calls=%async_computation.10 | async-start | bytes 8388608
  59.0 10.2 %slice-start.2 = ((s8[10485760]{0:T(1024)(128)(4,1)}), s8[4194304]{0:T(1024)(128)(4,1)S(1)}, s32[]{:S(2)}) async-start(s8[10485760]{0:T(1024)(128)(4,1)} %bitcast.350), calls=%async_computation.11 | async-start | bytes 8388608
  59.0 10.2 %copy-start.13 = (bf16[3,5120,128]{1,2,0:T(8,128)(2,1)S(1)}, bf16[3,5120,128]{1,2,0:T(8,128)(2,1)}, u32[]{:S(2)}) copy-start(bf16[3,5120,128]{1,2,0:T(8,128)(2,1)} %copy.20) | copy-start | bytes 11796484
  73.6 7.5 copy-start.11
  87.5 11.7 %copy-start.10 = (f32[1024,384]{0,1:S(1)}, f32[1024,384]{0,1}, u32[]{:S(2)}) copy-start(f32[1024,384]{0,1} %copy-done.9) | copy-start | bytes 4718596
  112.1 444.9 %reduce-scatter.8.cloned.1.call-start = ((), (), s32[]{:S(2)}) async-start(), calls=%async_computation.8 | async-start | bytes 1638400 | tf_op jit(solution)/shard_map/reduce_scatter | solution.py:241
  482.1 14.0 %copy-start.22 = (bf16[128,5120]{1,0:T(8,128)(2,1)S(1)}, bf16[128,5120]{1,0:T(8,128)(2,1)}, u32[]{:S(2)}) copy-start(bf16[128,5120]{1,0:T(8,128)(2,1)} %param.27) | copy-start | bytes 3932164
  512.8 7.1 slice-start.3
  512.8 71.3 %reduce-scatter.6.cloned.1.call-start = ((), (), s32[]{:S(2)}) async-start(), calls=%async_computation.7 | async-start | bytes 4915200 | tf_op jit(solution)/shard_map/reduce_scatter | solution.py:233
  516.4 5.4 slice-start.5
  528.1 247.3 %all-reduce.5.cloned.1.call-start = ((), (), s32[]{:S(2)}) async-start(), calls=%async_computation.5 | async-start | bytes 10485760 | tf_op jit(solution)/shard_map/psum | solution.py:207
  791.4 13.3 %copy-start.1 = (bf16[128,5120]{1,0:T(8,128)(2,1)S(1)}, bf16[128,5120]{1,0:T(8,128)(2,1)}, u32[]{:S(2)}) copy-start(bf16[128,5120]{1,0:T(8,128)(2,1)} %param.23) | copy-start | bytes 3932164
  (22 other events, 55.5 us)
Sparse Core Ops, SparseCore 0:
  10.4 132.5 all-gather.1
  145.3 167.4 reduce-scatter.3
  512.9 25.4 reduce-scatter.7
  541.4 42.7 reduce-scatter.5
  586.4 188.9 all-reduce.4
Sparse Core Ops, SparseCore 1:
  52.6 429.5 all-reduce.2
where the time goes:
time: 821 us; the launch traced here: 812 us
  waiting for transfers between devices  584 us (71%)
  matrix products  91.8 us (11%)
  other arithmetic  90.4 us (11%)
  local copies, waits for them, and re-layouts  21 us (3%)
  between operations  19.2 us (2%)
    psum x1, waiting for transfers between devices, body(): lax.psum(fake_local.astype(jnp.bfloat16), ('branch', 'seq'))  339 us
    psum x1, waiting for transfers between devices, body(): lax.psum(guided_seq, 'branch').astype(jnp.float32)  188 us
    all_gather x1, waiting for transfers between devices, body(): lax.all_gather(generated, 'seq', axis=1, tiled=True).astype(jnp.float32)  30.1 us
    reduce_scatter x1, waiting for transfers between devices, body(): lax.psum_scatter(head_backward(critic_normed, grad_attn, saved_state, cri...  25.3 us
    unnamed x3, matrix products  21.2 us
    unnamed x83, local copies, waits for them, and re-layouts  21 us
    dot_general x3, matrix products, head_forward(): jnp.einsum('bqhe,bkhe->bhqk', rope_query, rope_key, preferred_element_typ...  16.9 us
  transfers between devices with their start and end apart: 6, of which 4 were waited for; matrix products, arithmetic and copies ran while one was open for 21% of the time, Pallas kernels for 0%

commit v1 on v0

--- a/solution.py
+++ b/solution.py
@@ -9,6 +9,7 @@
 guidance = 5.0
 score_scale = 128.0 ** (-0.5)
 norm_eps = 1e-06
+matrix_derive = lambda ax_name, payload: lax.all_gather(payload, ax_name).sum(axis=0)
 
 
 def rope_tables(first_token):
@@ -204,7 +205,7 @@
         scatter_dimension=0,
         tiled=True,
     )
-    guided_rows = jnp.transpose(lax.psum(guided_seq, "branch").astype(jnp.float32), (1, 0, 2))
+    guided_rows = jnp.transpose(matrix_derive("branch", guided_seq).astype(jnp.float32), (1, 0, 2))
     fake_local = jnp.einsum(
         "bsc,cd->bsd", fake_attn, critic_out, preferred_element_type=jnp.float32
     )

time: 821 us -> 1000 us (1.22)
  waiting for transfers between devices: 584 us -> 751 us
  other arithmetic: 90.4 us -> 105 us
    all_gather x0 -> x1, waiting for transfers between devices: none -> 355 us  [lax.all_gather(payload, ax_name).sum(axis=0)]
    psum x1 -> x0, waiting for transfers between devices: 188 us -> none  [body(): lax.psum(guided_seq, 'branch').astype(jnp.float32)]
    reduce_sum x0 -> x1, other arithmetic: none -> 15 us  [lax.all_gather(payload, ax_name).sum(axis=0)]
  transfers between devices with their start and end apart: 6 -> 6, of which waited for: 4 -> 4; matrix products, arithmetic and copies ran while one was open for 21% -> 18% of each run, Pallas kernels for 0% -> 0%
where the time goes in v1:
time: 1000 us; the launch traced here: 995 us
  waiting for transfers between devices  751 us (75%)
  other arithmetic  105 us (10%)
  matrix products  91.9 us (9%)
  local copies, waits for them, and re-layouts  20.9 us (2%)
  between operations  19.2 us (2%)
    all_gather x1, waiting for transfers between devices, lax.all_gather(payload, ax_name).sum(axis=0)  355 us
    psum x1, waiting for transfers between devices, body(): lax.psum(fake_local.astype(jnp.bfloat16), ('branch', 'seq'))  339 us
    all_gather x1, waiting for transfers between devices, body(): lax.all_gather(generated, 'seq', axis=1, tiled=True).astype(jnp.float32)  30 us
    reduce_scatter x1, waiting for transfers between devices, body(): lax.psum_scatter(head_backward(critic_normed, grad_attn, saved_state, cri...  25.3 us
    unnamed x3, matrix products  21.2 us
    unnamed x83, local copies, waits for them, and re-layouts  20.9 us
  transfers between devices with their start and end apart: 6, of which 4 were waited for; matrix products, arithmetic and copies ran while one was open for 18% of the time, Pallas kernels for 0%

profile of v1, /device:TPU:0, one launch (start us, length us, event | category | flops | bytes accessed | tf_op | source)
XLA Modules:
  0.0 994.6 jit_solution(12937940880460334313)
XLA Ops:
  10.1 6.3 copy.18
  16.6 11.9 %multiply_reduce_fusion = (f32[1024]{0:T(1024)S(1)}, f32[1024]{0:T(1024)S(1)}) fusion(bf16[1,1024,5120]{2,1,0:T(8,128)(2,1)} %param.15, f32[5120]{0:T(1024)S(1)} %convert_element_type.350, f32[5120]{0:T(1024)S(1)} %bitcast.387), kind=kLoop, calls=%fused_computation.3 | loop fusion | flops 36698112 | bytes 10534912 | tf_op jit(solution)/shard_map/reduce_sum | solution.py:51
  28.5 6.9 fusion.12
  38.7 4.3 fusion.28
  46.6 5.8 convert_bitcast_fusion
  52.5 6.4 copy.20
  59.0 10.0 %fusion.5 = f32[1024,384]{0,1:S(1)} fusion(bf16[5120,384]{0,1:T(8,128)(2,1)} %bitcast.385, bf16[1,1024,5120]{2,1,0:T(8,128)(2,1)} %param.15, f32[1024]{0:T(1024)S(1)} %add_rsqrt_fusion.2, f32[5120]{0:T(1024)S(1)} %convert_element_type.350, f32[5120]{0:T(1024)S(1)} %copy-done.31), kind=kOutput, calls=%fused_computation.12 | convolution fusion | flops 4052746240 | bytes 16035840
  69.2 4.3 fusion.2
  74.8 6.2 fusion.30
  81.1 6.4 fusion.29
  87.5 11.7 %fusion.38 = f32[1024,5120]{1,0:T(8,128)} fusion(bf16[128,5120]{1,0:T(8,128)(2,1)S(1)} %copy-done, f32[1024,1024]{0,1:T(8,128)} %get-tuple-element.54, f32[1024]{0:T(1024)S(1)} %get-tuple-element.53, f32[3,1,1024,128]{2,3,1,0:T(8,128)} %bitcast.383), kind=kOutput, calls=%fused_computation.57 | convolution fusion | flops 1613889536 | bytes 26742784 | tf_op jit(solution)/shard_map/bsc,cd->sbd/dot_general | solution.py:196
  99.2 12.9 %fusion.20 = bf16[1024,1,5120]{2,0,1:T(8,128)(2,1)} fusion(bf16[128,5120]{1,0:T(8,128)(2,1)S(1)} %copy-done, f32[1024,5120]{1,0:T(8,128)} %fusion.38, f32[1024,1024]{0,1:T(8,128)} %get-tuple-element.56, f32[1024]{0:T(1024)S(1)} %get-tuple-element.55, f32[3,1,1024,128]{2,3,1,0:T(8,128)S(1)} %bitcast.379), kind=kOutput, calls=%fused_computation.30 | convolution fusion | flops 1634861056 | bytes 37228544 | tf_op jit(solution)/shard_map/bsc,cd->sbd/dot_general | solution.py:199
  113.0 30.0 %all-gather.4.cloned.1.call-done = bf16[1,1024,5120]{2,1,0:T(8,128)(2,1)} async-done(((bf16[1,512,5120]{2,1,0:T(8,128)(2,1)}), bf16[1,1024,5120]{2,1,0:T(8,128)(2,1)}) %all-gather.4.cloned.1.call-update) | async-done | bytes 10485776 | tf_op jit(solution)/shard_map/all_gather | solution.py:213
  143.0 339.1 %all-reduce.2.cloned.1.call-done = bf16[1,1024,5120]{2,1,0:T(8,128)(2,1)} async-done(((bf16[1,1024,5120]{2,1,0:T(8,128)(2,1)}), bf16[1,1024,5120]{2,1,0:T(8,128)(2,1)}) %all-reduce.2.cloned.1.call-update) | async-done | bytes 10485776 | tf_op jit(solution)/shard_map/psum | solution.py:212
  482.1 13.9 %fusion.7 = bf16[1024,5120]{1,0:T(8,128)(2,1)S(1)} fusion(bf16[1,1024,5120]{2,1,0:T(8,128)(2,1)} %all-gather.4.cloned.1.call-done, bf16[1,1024,5120]{2,1,0:T(8,128)(2,1)} %param.15, f32[]{:T(128)} %bitcast, f32[]{:T(128)} %bitcast.93, f32[5120]{0:T(1024)S(1)} %bitcast.390, bf16[1,1024,5120]{2,1,0:T(8,128)(2,1)} %all-reduce.2.cloned.1.call-done), kind=kLoop, calls=%fused_computation.13 | loop fusion | flops 57671680 | bytes 41963528 | tf_op jit(solution)/shard_map/reshape.74
  521.8 6.2 fusion.24
  528.7 13.9 %convert_element_type.333 = f32[1,1024,5120]{2,1,0:T(8,128)} convert(bf16[1,1024,5120]{2,1,0:T(8,128)(2,1)} %param.15) | non-fusion elementwise | flops 5242880 | bytes 31457280 | tf_op jit(solution)/shard_map/convert_element_type | solution.py:179
  542.5 14.5 %convert_element_type.349 = f32[1,1024,5120]{2,1,0:T(8,128)} convert(bf16[1,1024,5120]{2,1,0:T(8,128)(2,1)} %all-reduce.2.cloned.1.call-done) | non-fusion elementwise | flops 5242880 | bytes 31457280 | tf_op jit(solution)/shard_map/convert_element_type | solution.py:212
  558.9 25.3 %reduce-scatter.6.cloned.1.call-done = bf16[3,1280,128]{1,2,0:T(8,128)(2,1)} async-done(((bf16[3,5120,128]{1,2,0:T(8,128)(2,1)}), bf16[3,1280,128]{1,2,0:T(8,128)(2,1)}) %reduce-scatter.6.cloned.1.call-update) | async-done | bytes 983056 | tf_op jit(solution)/shard_map/reduce_scatter | solution.py:234
  587.0 355.5 %all-gather.6.cloned.1.call-done = bf16[2048,1,5120]{2,0,1:T(8,128)(2,1)} async-done(((bf16[512,1,5120]{2,0,1:T(8,128)(2,1)}), bf16[2048,1,5120]{2,0,1:T(8,128)(2,1)}) %all-gather.6.cloned.1.call-update) | async-done | bytes 20971536 | tf_op jit(solution)/shard_map/all_gather | solution.py:12
  942.5 15.0 %reduce.21 = bf16[512,5120]{1,0:T(8,128)(2,1)} reduce(bf16[4,512,5120]{2,1,0:T(8,128)(2,1)} %bitcast.375, bf16[]{:T(256)} %constant.91.clone.1), dimensions={0}, to_apply=%region_13.14 | reduce | flops 7864320 | bytes 26214402 | tf_op jit(solution)/shard_map/reduce_sum | solution.py:12
  957.5 9.9 abs_reduce_fusion
  967.4 5.6 psum.15
  973.7 13.3 %divide_convert_fusion = bf16[1,512,5120]{2,1,0:T(8,128)(2,1)} fusion(f32[1,1024,5120]{2,1,0:T(8,128)} %convert_element_type.349, s32[]{:T(128)S(6)} %select_n.143, f32[1,1024,5120]{2,1,0:T(8,128)} %convert_element_type.333, f32[]{:T(128)} %bitcast.89, f32[5120]{0:T(1024)S(1)} %bitcast.393, f32[]{:T(128)} %bitcast, bf16[512,5120]{1,0:T(8,128)(2,1)} %reduce.21, ...), kind=kLoop, calls=%fused_computation.21 | loop fusion | flops 39321600 | bytes 31498252 | tf_op jit(solution)/shard_map/convert_element_type | solution.py:230
  (139 shorter events, 39.8 us)
Async XLA Ops:
  8.0 79.5 %copy-start = (bf16[128,5120]{1,0:T(8,128)(2,1)S(1)}, bf16[128,5120]{1,0:T(8,128)(2,1)}, u32[]{:S(2)}) copy-start(bf16[128,5120]{1,0:T(8,128)(2,1)} %param.23) | copy-start | bytes 3932164
  8.0 134.9 %all-gather.4.cloned.1.call-start = ((), (), s32[]{:S(2)}) async-start(), calls=%async_computation.5 | async-start | bytes 15728640 | tf_op jit(solution)/shard_map/all_gather | solution.py:213
  8.8 7.7 copy-start.28
  8.8 473.3 %all-reduce.2.cloned.1.call-start = ((), (), s32[]{:S(2)}) async-start(), calls=%async_computation.3 | async-start | bytes 20971520 | tf_op jit(solution)/shard_map/psum | solution.py:212
  16.6 11.9 %copy-start.2 = (bf16[1,1024,5120]{2,1,0:T(8,128)(2,1)S(1)}, bf16[1,1024,5120]{2,1,0:T(8,128)(2,1)}, u32[]{:S(2)}) copy-start(bf16[1,1024,5120]{2,1,0:T(8,128)(2,1)} %param.15) | copy-start | bytes 31457284
  16.6 11.9 %copy-start.32 = (f32[5120]{0:T(1024)S(1)}, f32[5120]{0:T(1024)}, u32[]{:S(2)}) copy-start(f32[5120]{0:T(1024)} %param.28) | copy-start | bytes 61444
  28.5 7.0 copy-start.29
  35.4 7.6 copy-start.3
  36.8 6.3 copy-start.7
  52.5 6.5 copy-start.31
  52.5 475.7 %reduce-scatter.4.cloned.1.call-start = ((), (), s32[]{:S(2)}) async-start(), calls=%async_computation.4 | async-start | bytes 15728640 | tf_op jit(solution)/shard_map/reduce_scatter | solution.py:202
  52.5 16.6 %slice-start = ((s8[10485760]{0:T(1024)(128)(4,1)}), s8[2097152]{0:T(1024)(128)(4,1)S(1)}, s32[]{:S(2)}) async-start(s8[10485760]{0:T(1024)(128)(4,1)} %bitcast.357), calls=%async_computation.9 | async-start | bytes 4194304
  59.0 10.2 %slice-start.1 = ((s8[10485760]{0:T(1024)(128)(4,1)}), s8[4194304]{0:T(1024)(128)(4,1)S(1)}, s32[]{:S(2)}) async-start(s8[10485760]{0:T(1024)(128)(4,1)} %bitcast.357), calls=%async_computation.10 | async-start | bytes 8388608
  59.0 10.2 %slice-start.2 = ((s8[10485760]{0:T(1024)(128)(4,1)}), s8[4194304]{0:T(1024)(128)(4,1)S(1)}, s32[]{:S(2)}) async-start(s8[10485760]{0:T(1024)(128)(4,1)} %bitcast.357), calls=%async_computation.11 | async-start | bytes 8388608
  59.0 10.2 %copy-start.13 = (bf16[3,5120,128]{1,2,0:T(8,128)(2,1)S(1)}, bf16[3,5120,128]{1,2,0:T(8,128)(2,1)}, u32[]{:S(2)}) copy-start(bf16[3,5120,128]{1,2,0:T(8,128)(2,1)} %copy.20) | copy-start | bytes 11796484
  73.5 7.6 copy-start.11
  87.5 11.7 %copy-start.10 = (f32[1024,384]{0,1:S(1)}, f32[1024,384]{0,1}, u32[]{:S(2)}) copy-start(f32[1024,384]{0,1} %copy-done.9) | copy-start | bytes 4718596
  112.2 444.8 %reduce-scatter.8.cloned.1.call-start = ((), (), s32[]{:S(2)}) async-start(), calls=%async_computation.7 | async-start | bytes 1638400 | tf_op jit(solution)/shard_map/reduce_scatter | solution.py:242
  482.1 14.0 %copy-start.22 = (bf16[128,5120]{1,0:T(8,128)(2,1)S(1)}, bf16[128,5120]{1,0:T(8,128)(2,1)}, u32[]{:S(2)}) copy-start(bf16[128,5120]{1,0:T(8,128)(2,1)} %param.27) | copy-start | bytes 3932164
  512.8 7.1 slice-start.3
  512.8 71.4 %reduce-scatter.6.cloned.1.call-start = ((), (), s32[]{:S(2)}) async-start(), calls=%async_computation.6 | async-start | bytes 4915200 | tf_op jit(solution)/shard_map/reduce_scatter | solution.py:234
  516.4 5.4 slice-start.5
  528.1 414.4 %all-gather.6.cloned.1.call-start = ((), (), s32[]{:S(2)}) async-start(), calls=%async_computation.8 | async-start | bytes 26214400 | tf_op jit(solution)/shard_map/all_gather | solution.py:12
  973.7 13.3 %copy-start.1 = (bf16[128,5120]{1,0:T(8,128)(2,1)S(1)}, bf16[128,5120]{1,0:T(8,128)(2,1)}, u32[]{:S(2)}) copy-start(bf16[128,5120]{1,0:T(8,128)(2,1)} %param.23) | copy-start | bytes 3932164
  (22 other events, 55.5 us)
Sparse Core Ops, SparseCore 0:
  10.4 132.5 all-gather.3
  145.3 167.4 reduce-scatter.3
  513.0 25.4 reduce-scatter.7
  541.4 42.7 reduce-scatter.5
  585.6 356.7 all-gather.5
Sparse Core Ops, SparseCore 1:
  52.5 429.5 all-reduce.1
